TPU v7x, 32 devices: a whole 2x2x4 slice. The times are simulated.
32 devices in a mesh: col: 8 (over y, x, core), row: 4 (over z).
Axes of the slice: x: 2, y: 2, z: 4, core: 2. Of those that a mesh axis runs over, the one named last changes fastest.
Arguments:
- matrix: float32 [16, 512, 4096], P(None, 'row', 'col'), may hold values from -0.4 to 2.4, as said below
- pivots: int32 [8, 512], replicated, may hold values from 0 to 511, as said below
- seeds: float32 [8, 512, 512], P('col'), may hold values from -1 to 2, as said below
Outputs:
- factors: float32 [16, 512, 4096], P(None, 'row', 'col')
Inputs may be any that keep to these rules, and one draw needn't show every extreme that they name: Each row of pivots is an ordering of 0 .. 511. Block (r, j) of matrix is zero where r and j differ by more than 8. seeds[k] approximates the inverse of block (k, k) of matrix after the replacement of rows by pivots[k].
All inputs are finite; a program needn't handle non-finite values.
Results may differ from a plain program's by a relative error of at most 0.0001.
Values sent between devices are 32-bit elements; how exact they have to be, the bound alone decides.
A program may use at most 64 MiB of HBM per device.

v0:
```python
import jax
import jax.numpy as jnp
from jax import lax
from jax.sharding import PartitionSpec as P

HB = 8
SWEEPS = 2


def from_root(block, axis, source):
    block = jnp.where(lax.axis_index(axis) == source, block, jnp.zeros_like(block))
    return lax.psum(block, axis)


def dot_high(left, right):
    return jnp.dot(left, right, precision=lax.Precision.HIGHEST, preferred_element_type=jnp.float32)


def refine(pivot_block, approx, identity):
    for sweep_index in range(SWEEPS):
        approx = dot_high(approx, 2.0 * identity - dot_high(pivot_block, approx))
    return approx


def local(matrix, pivots, seeds):
    col_count = lax.axis_size("col")
    col_index = lax.axis_index("col")
    row_index = lax.axis_index("row")
    row_share = matrix.shape[1]
    panel_width = matrix.shape[2]
    identity = jnp.eye(panel_width, dtype=jnp.float32)
    seed_block = seeds[0]

    def eliminate(panel_index, factors):
        local_row = lax.dynamic_index_in_dim(factors, panel_index, 0, keepdims=False)
        block_row = lax.all_gather(local_row, "row", axis=0, tiled=True)
        ordering = lax.dynamic_index_in_dim(pivots, panel_index, 0, keepdims=False)
        swapped = jnp.take(block_row, ordering, axis=0)
        block_row = jnp.where(col_index >= panel_index, swapped, block_row)
        local_row = lax.dynamic_slice_in_dim(block_row, row_index * row_share, row_share, 0)
        factors = lax.dynamic_update_index_in_dim(factors, local_row, panel_index, 0)
        is_owner = col_index == panel_index
        approx = lax.cond(
            is_owner, lambda: refine(block_row, seed_block, identity), lambda: seed_block
        )
        below_rows = lax.dynamic_slice_in_dim(factors, panel_index + 1, HB, 0)
        below_flat = below_rows.reshape(HB * row_share, panel_width)
        scaled = lax.cond(is_owner, lambda: dot_high(below_flat, approx), lambda: below_flat)
        in_reach = (col_index > panel_index) & (col_index <= panel_index + HB)
        arrived = from_root(scaled, "col", panel_index)
        updated = below_flat - dot_high(arrived, block_row)
        result = jnp.where(is_owner, scaled, jnp.where(in_reach, updated, below_flat))
        return lax.dynamic_update_slice_in_dim(
            factors, result.reshape(HB, row_share, panel_width), panel_index + 1, 0
        )

    return lax.fori_loop(0, col_count, eliminate, matrix)


def solution(mesh):
    return jax.shard_map(
        local,
        mesh=mesh,
        in_specs=(P(None, "row", "col"), P(), P("col", None, None)),
        out_specs=P(None, "row", "col"),
        check_vma=False,
    )
```

profile of v0, /device:TPU:0, one launch (start us, length us, event | category | flops | bytes accessed | tf_op | source)
XLA Modules:
  0.0 1028.8 jit_solution(17869282881997952237)
XLA Ops:
  11.4 1010.8 %while.17 = (s32[]{:T(128)}, f32[16,128,512]{2,1,0:T(8,128)}, s32[]{:T(128)}, s32[8,512]{1,0:T(8,128)}, s32[]{:T(128)}, /*index=5*/f32[512,512]{1,0:T(8,128)S(1)...) while((s32[]{:T(128)}, f32[16,128,512]{2,1,0:T(8,128)}, ...), condition=%wide.region_6.7_spmd.clone.clone, body=%wide.region_0.6_spmd.clone.clone.sunk | while | flops 12889626624 | bytes 111953976 | solution.py:57
  15.0 29.5 %all-gather.6.cloned.1.call-done = f32[1,512,512]{2,1,0:T(8,128)} async-done(((f32[1,128,512]{2,1,0:T(8,128)}), f32[1,512,512]{2,1,0:T(8,128)}) %all-gather.6.cloned.1.call-update) | async-done | bytes 1048592 | tf_op jit(solution)/shard_map/while/body/eval_jaxpr/all_gather | solution.py:36
  50.7 11.3 %conditional.8 = (f32[512,512]{1,0:T(8,128)}) conditional(s32[]{:T(128)} %convert_element_type.27, f32[512,512]{1,0:T(8,128)S(1)} %get-tuple-element.345, (f32[512,512]{1,0:T(8,128)}, f32[512,512]{1,0:T(8,128)}, f32[512,512]{1,0:T(8,128)S(1)}, f32[512,512]{1,0:T(8,128)S(1)}) %tuple.77), branch_computations={%region_1.1_spmd, %region_2.2_spmd} | conditional | flops 6443499520 | bytes 18874404 | solution.py:43
  63.9 6.0 conditional.9
  63.9 6.0 fusion.5
  73.1 59.5 %all-reduce.2.cloned.1.call-done = f32[1024,512]{1,0:T(8,128)} async-done(((f32[1024,512]{1,0:T(8,128)}), f32[1024,512]{1,0:T(8,128)}) %all-reduce.2.cloned.1.call-update) | async-done | bytes 2097168 | tf_op jit(solution)/shard_map/while/body/eval_jaxpr/psum | solution.py:12
  132.6 5.9 fusion.27
  144.4 25.8 %all-gather.6.cloned.1.call-done = f32[1,512,512]{2,1,0:T(8,128)} async-done(((f32[1,128,512]{2,1,0:T(8,128)}), f32[1,512,512]{2,1,0:T(8,128)}) %all-gather.6.cloned.1.call-update) | async-done | bytes 1048592 | tf_op jit(solution)/shard_map/while/body/eval_jaxpr/all_gather | solution.py:36
  182.2 75.3 %all-reduce.2.cloned.1.call-done = f32[1024,512]{1,0:T(8,128)} async-done(((f32[1024,512]{1,0:T(8,128)}), f32[1024,512]{1,0:T(8,128)}) %all-reduce.2.cloned.1.call-update) | async-done | bytes 2097168 | tf_op jit(solution)/shard_map/while/body/eval_jaxpr/psum | solution.py:12
  257.5 5.3 fusion.27
  268.7 25.5 %all-gather.6.cloned.1.call-done = f32[1,512,512]{2,1,0:T(8,128)} async-done(((f32[1,128,512]{2,1,0:T(8,128)}), f32[1,512,512]{2,1,0:T(8,128)}) %all-gather.6.cloned.1.call-update) | async-done | bytes 1048592 | tf_op jit(solution)/shard_map/while/body/eval_jaxpr/all_gather | solution.py:36
  306.2 76.9 %all-reduce.2.cloned.1.call-done = f32[1024,512]{1,0:T(8,128)} async-done(((f32[1024,512]{1,0:T(8,128)}), f32[1024,512]{1,0:T(8,128)}) %all-reduce.2.cloned.1.call-update) | async-done | bytes 2097168 | tf_op jit(solution)/shard_map/while/body/eval_jaxpr/psum | solution.py:12
  394.4 26.3 %all-gather.6.cloned.1.call-done = f32[1,512,512]{2,1,0:T(8,128)} async-done(((f32[1,128,512]{2,1,0:T(8,128)}), f32[1,512,512]{2,1,0:T(8,128)}) %all-gather.6.cloned.1.call-update) | async-done | bytes 1048592 | tf_op jit(solution)/shard_map/while/body/eval_jaxpr/all_gather | solution.py:36
  432.6 76.5 %all-reduce.2.cloned.1.call-done = f32[1024,512]{1,0:T(8,128)} async-done(((f32[1024,512]{1,0:T(8,128)}), f32[1024,512]{1,0:T(8,128)}) %all-reduce.2.cloned.1.call-update) | async-done | bytes 2097168 | tf_op jit(solution)/shard_map/while/body/eval_jaxpr/psum | solution.py:12
  520.3 25.8 %all-gather.6.cloned.1.call-done = f32[1,512,512]{2,1,0:T(8,128)} async-done(((f32[1,128,512]{2,1,0:T(8,128)}), f32[1,512,512]{2,1,0:T(8,128)}) %all-gather.6.cloned.1.call-update) | async-done | bytes 1048592 | tf_op jit(solution)/shard_map/while/body/eval_jaxpr/all_gather | solution.py:36
  558.2 76.9 %all-reduce.2.cloned.1.call-done = f32[1024,512]{1,0:T(8,128)} async-done(((f32[1024,512]{1,0:T(8,128)}), f32[1024,512]{1,0:T(8,128)}) %all-reduce.2.cloned.1.call-update) | async-done | bytes 2097168 | tf_op jit(solution)/shard_map/while/body/eval_jaxpr/psum | solution.py:12
  646.3 26.3 %all-gather.6.cloned.1.call-done = f32[1,512,512]{2,1,0:T(8,128)} async-done(((f32[1,128,512]{2,1,0:T(8,128)}), f32[1,512,512]{2,1,0:T(8,128)}) %all-gather.6.cloned.1.call-update) | async-done | bytes 1048592 | tf_op jit(solution)/shard_map/while/body/eval_jaxpr/all_gather | solution.py:36
  684.6 76.5 %all-reduce.2.cloned.1.call-done = f32[1024,512]{1,0:T(8,128)} async-done(((f32[1024,512]{1,0:T(8,128)}), f32[1024,512]{1,0:T(8,128)}) %all-reduce.2.cloned.1.call-update) | async-done | bytes 2097168 | tf_op jit(solution)/shard_map/while/body/eval_jaxpr/psum | solution.py:12
  761.0 5.3 fusion.27
  772.2 25.8 %all-gather.6.cloned.1.call-done = f32[1,512,512]{2,1,0:T(8,128)} async-done(((f32[1,128,512]{2,1,0:T(8,128)}), f32[1,512,512]{2,1,0:T(8,128)}) %all-gather.6.cloned.1.call-update) | async-done | bytes 1048592 | tf_op jit(solution)/shard_map/while/body/eval_jaxpr/all_gather | solution.py:36
  810.1 77.8 %all-reduce.2.cloned.1.call-done = f32[1024,512]{1,0:T(8,128)} async-done(((f32[1024,512]{1,0:T(8,128)}), f32[1024,512]{1,0:T(8,128)}) %all-reduce.2.cloned.1.call-update) | async-done | bytes 2097168 | tf_op jit(solution)/shard_map/while/body/eval_jaxpr/psum | solution.py:12
  899.1 26.2 %all-gather.6.cloned.1.call-done = f32[1,512,512]{2,1,0:T(8,128)} async-done(((f32[1,128,512]{2,1,0:T(8,128)}), f32[1,512,512]{2,1,0:T(8,128)}) %all-gather.6.cloned.1.call-update) | async-done | bytes 1048592 | tf_op jit(solution)/shard_map/while/body/eval_jaxpr/all_gather | solution.py:36
  937.3 77.4 %all-reduce.2.cloned.1.call-done = f32[1024,512]{1,0:T(8,128)} async-done(((f32[1024,512]{1,0:T(8,128)}), f32[1024,512]{1,0:T(8,128)}) %all-reduce.2.cloned.1.call-update) | async-done | bytes 2097168 | tf_op jit(solution)/shard_map/while/body/eval_jaxpr/psum | solution.py:12
  1014.7 5.3 fusion.27
  (225 shorter events, 195.4 us)
Async XLA Ops:
  11.4 33.1 %all-gather.6.cloned.1.call-start = ((), (), s32[]{:S(2)}) async-start(), calls=%async_computation | async-start | bytes 1310720 | tf_op jit(solution)/shard_map/while/body/eval_jaxpr/all_gather | solution.py:36
  13.1 119.4 %all-reduce.2.cloned.1.call-start = ((), (), s32[]{:S(2)}) async-start(), calls=%async_computation.1 | async-start | bytes 4194304 | tf_op jit(solution)/shard_map/while/body/eval_jaxpr/psum | solution.py:12
  132.6 5.9 copy-start.4
  140.8 29.4 %all-gather.6.cloned.1.call-start = ((), (), s32[]{:S(2)}) async-start(), calls=%async_computation | async-start | bytes 1310720 | tf_op jit(solution)/shard_map/while/body/eval_jaxpr/all_gather | solution.py:36
  142.5 115.0 %all-reduce.2.cloned.1.call-start = ((), (), s32[]{:S(2)}) async-start(), calls=%async_computation.1 | async-start | bytes 4194304 | tf_op jit(solution)/shard_map/while/body/eval_jaxpr/psum | solution.py:12
  257.5 5.3 copy-start.4
  265.1 29.1 %all-gather.6.cloned.1.call-start = ((), (), s32[]{:S(2)}) async-start(), calls=%async_computation | async-start | bytes 1310720 | tf_op jit(solution)/shard_map/while/body/eval_jaxpr/all_gather | solution.py:36
  266.8 116.4 %all-reduce.2.cloned.1.call-start = ((), (), s32[]{:S(2)}) async-start(), calls=%async_computation.1 | async-start | bytes 4194304 | tf_op jit(solution)/shard_map/while/body/eval_jaxpr/psum | solution.py:12
  383.2 5.3 copy-start.4
  390.8 29.9 %all-gather.6.cloned.1.call-start = ((), (), s32[]{:S(2)}) async-start(), calls=%async_computation | async-start | bytes 1310720 | tf_op jit(solution)/shard_map/while/body/eval_jaxpr/all_gather | solution.py:36
  392.4 116.7 %all-reduce.2.cloned.1.call-start = ((), (), s32[]{:S(2)}) async-start(), calls=%async_computation.1 | async-start | bytes 4194304 | tf_op jit(solution)/shard_map/while/body/eval_jaxpr/psum | solution.py:12
  509.1 5.3 copy-start.4
  516.7 29.5 %all-gather.6.cloned.1.call-start = ((), (), s32[]{:S(2)}) async-start(), calls=%async_computation | async-start | bytes 1310720 | tf_op jit(solution)/shard_map/while/body/eval_jaxpr/all_gather | solution.py:36
  518.4 116.7 %all-reduce.2.cloned.1.call-start = ((), (), s32[]{:S(2)}) async-start(), calls=%async_computation.1 | async-start | bytes 4194304 | tf_op jit(solution)/shard_map/while/body/eval_jaxpr/psum | solution.py:12
  635.1 5.3 copy-start.4
  642.7 29.9 %all-gather.6.cloned.1.call-start = ((), (), s32[]{:S(2)}) async-start(), calls=%async_computation | async-start | bytes 1310720 | tf_op jit(solution)/shard_map/while/body/eval_jaxpr/all_gather | solution.py:36
  644.4 116.7 %all-reduce.2.cloned.1.call-start = ((), (), s32[]{:S(2)}) async-start(), calls=%async_computation.1 | async-start | bytes 4194304 | tf_op jit(solution)/shard_map/while/body/eval_jaxpr/psum | solution.py:12
  761.0 5.3 copy-start.4
  768.6 29.5 %all-gather.6.cloned.1.call-start = ((), (), s32[]{:S(2)}) async-start(), calls=%async_computation | async-start | bytes 1310720 | tf_op jit(solution)/shard_map/while/body/eval_jaxpr/all_gather | solution.py:36
  770.3 117.6 %all-reduce.2.cloned.1.call-start = ((), (), s32[]{:S(2)}) async-start(), calls=%async_computation.1 | async-start | bytes 4194304 | tf_op jit(solution)/shard_map/while/body/eval_jaxpr/psum | solution.py:12
  887.9 5.3 copy-start.4
  895.5 29.8 %all-gather.6.cloned.1.call-start = ((), (), s32[]{:S(2)}) async-start(), calls=%async_computation | async-start | bytes 1310720 | tf_op jit(solution)/shard_map/while/body/eval_jaxpr/all_gather | solution.py:36
  897.2 117.5 %all-reduce.2.cloned.1.call-start = ((), (), s32[]{:S(2)}) async-start(), calls=%async_computation.1 | async-start | bytes 4194304 | tf_op jit(solution)/shard_map/while/body/eval_jaxpr/psum | solution.py:12
  1014.7 5.3 copy-start.4
  (26 other events, 75.5 us)
Sparse Core Ops, SparseCore 0:
  13.8 30.6 all-gather.5
  73.2 59.3 all-reduce.1
  143.1 26.9 all-gather.5
  182.3 75.1 all-reduce.1
  267.1 27.0 all-gather.5
  306.3 76.7 all-reduce.1
  393.1 27.4 all-gather.5
  432.7 76.3 all-reduce.1
  519.1 27.0 all-gather.5
  558.3 76.7 all-reduce.1
  645.1 27.4 all-gather.5
  684.7 76.3 all-reduce.1
  771.0 27.0 all-gather.5
  810.2 77.6 all-reduce.1
  897.5 27.6 all-gather.5
  937.4 77.2 all-reduce.1
where the time goes:
time: 1030 us
  waiting for transfers between devices  808 us (78%)
  local copies, waits for them, and re-layouts  106 us (10%)
  matrix products  60 us (6%)
  other arithmetic  39.8 us (4%)
  between operations  13.1 us (1%)
    psum x8, waiting for transfers between devices, from_root(): return lax.psum(block, axis)  597 us
    all_gather x8, waiting for transfers between devices, eliminate(): block_row = lax.all_gather(local_row, 'row', axis=0, tiled=True)  211 us
    dot_general x13, matrix products, dot_high(): jnp.dot(left, right, precision=lax.Precision.HIGHEST, preferred_element_t...  60 us
    gather x8, local copies, waits for them, and re-layouts, eliminate(): swapped = jnp.take(block_row, ordering, axis=0)  32.5 us
  transfers between devices with their start and end apart: 16, of which 16 were waited for; matrix products, arithmetic and copies ran while one was open for 1% of the time, Pallas kernels for 0%

commit v1 on v0

--- a/solution.py
+++ b/solution.py
@@ -33,7 +33,20 @@
 
     def eliminate(panel_index, factors):
         local_row = lax.dynamic_index_in_dim(factors, panel_index, 0, keepdims=False)
-        block_row = lax.all_gather(local_row, "row", axis=0, tiled=True)
+
+        def perform_sheet(vals, net_axis="row"):
+            n_blocks = lax.axis_size(net_axis)
+            series = [vals]
+            for dev_i in range(n_blocks - 1):
+                response = lax.ppermute(
+                    series[-1], net_axis, [(c, (c + 1) % n_blocks) for c in range(n_blocks)]
+                )
+                series.append(response)
+            kept_arr = jnp.concatenate(series[::-1], axis=0)
+            formed = lax.axis_index(net_axis)
+            return jnp.roll(kept_arr, (formed + 1) * vals.shape[0], axis=0)
+
+        block_row = perform_sheet(local_row)
         ordering = lax.dynamic_index_in_dim(pivots, panel_index, 0, keepdims=False)
         swapped = jnp.take(block_row, ordering, axis=0)
         block_row = jnp.where(col_index >= panel_index, swapped, block_row)

time: 1030 us -> 970 us (0.942)
  waiting for transfers between devices: 808 us -> 740 us
  starting transfers between devices: 0.35 us -> 13.3 us
    all_gather x8 -> x0, waiting for transfers between devices: 211 us -> none  [eliminate(): block_row = lax.all_gather(local_row, 'row', axis=0, tiled=True)]
    ppermute x0 -> x24, waiting for transfers between devices: none -> 184 us  [perform_sheet(): lax.ppermute(series[-1], net_axis, [(c, (c + 1) % n_blocks) for c in rang...]
    psum x8, waiting for transfers between devices: 597 us -> 555 us  [from_root(): return lax.psum(block, axis)]
    gather x8, local copies, waits for them, and re-layouts: 32.5 us -> 18.8 us  [eliminate(): swapped = jnp.take(block_row, ordering, axis=0)]
    ppermute x0 -> x24, starting transfers between devices: none -> 13.3 us  [perform_sheet(): lax.ppermute(series[-1], net_axis, [(c, (c + 1) % n_blocks) for c in rang...]
    dynamic_slice x8, local copies, waits for them, and re-layouts: 13.4 us -> 0.55 us  [perform_sheet(): return jnp.roll(kept_arr, (formed + 1) * vals.shape[0], axis=0)]
  transfers between devices with their start and end apart: 16 -> 32, of which waited for: 16 -> 32; matrix products, arithmetic and copies ran while one was open for 1% -> 1% of each run, Pallas kernels for 0% -> 0%
where the time goes in v1:
time: 970 us; the launch traced here: 968 us
  waiting for transfers between devices  740 us (76%)
  local copies, waits for them, and re-layouts  108 us (11%)
  matrix products  57.5 us (6%)
  other arithmetic  34.3 us (4%)
  between operations  13.4 us (1%)
  starting transfers between devices  13.3 us (1%)
    psum x8, waiting for transfers between devices, from_root(): return lax.psum(block, axis)  555 us
    ppermute x24, waiting for transfers between devices, perform_sheet(): lax.ppermute(series[-1], net_axis, [(c, (c + 1) % n_blocks) for c in rang...  184 us
    dot_general x13, matrix products, dot_high(): jnp.dot(left, right, precision=lax.Precision.HIGHEST, preferred_element_t...  57.5 us
  transfers between devices with their start and end apart: 32, of which 32 were waited for; matrix products, arithmetic and copies ran while one was open for 1% of the time, Pallas kernels for 0%

profile of v1, /device:TPU:0, one launch (start us, length us, event | category | flops | bytes accessed | tf_op | source)
XLA Modules:
  0.0 967.8 jit_solution(9450157458917369624)
XLA Ops:
  11.4 949.5 %while.17 = (s32[]{:T(128)}, f32[16,128,512]{2,1,0:T(8,128)}, s32[]{:T(128)}, s32[8,512]{1,0:T(8,128)}, s32[]{:T(128)}, /*index=5*/f32[512,512]{1,0:T(8,128)S(1)...) while((s32[]{:T(128)}, f32[16,128,512]{2,1,0:T(8,128)}, ...), condition=%wide.region_6.7_spmd.clone.clone, body=%wide.region_0.6_spmd.clone.clone.sunk | while | flops 12889626624 | bytes 83904816 | solution.py:70
  15.5 8.3 collective-permute-done
  24.7 8.4 collective-permute-done.1
  33.2 8.3 collective-permute-done.2
  49.8 10.0 %conditional.8 = (f32[512,512]{1,0:T(8,128)}) conditional(s32[]{:T(128)} %convert_element_type.27, f32[512,512]{1,0:T(8,128)S(1)} %get-tuple-element.358, (f32[512,512]{1,0:T(8,128)S(1)}, f32[512,512]{1,0:T(8,128)S(1)}, f32[512,512]{1,0:T(8,128)S(1)}, f32[512,512]{1,0:T(8,128)S(1)}) %tuple.77), branch_computations={%region_1.1_spmd, %region_2.2_spmd} | conditional | flops 6443499520 | bytes 14680072 | solution.py:56
  70.9 57.8 %all-reduce.2.cloned.1.call-done = f32[1024,512]{1,0:T(8,128)} async-done(((f32[1024,512]{1,0:T(8,128)}), f32[1024,512]{1,0:T(8,128)}) %all-reduce.2.cloned.1.call-update) | async-done | bytes 2097168 | tf_op jit(solution)/shard_map/while/body/eval_jaxpr/psum | solution.py:12
  146.0 7.3 collective-permute-done.1
  153.4 8.1 collective-permute-done.2
  175.5 67.6 %all-reduce.2.cloned.1.call-done = f32[1024,512]{1,0:T(8,128)} async-done(((f32[1024,512]{1,0:T(8,128)}), f32[1024,512]{1,0:T(8,128)}) %all-reduce.2.cloned.1.call-update) | async-done | bytes 2097168 | tf_op jit(solution)/shard_map/while/body/eval_jaxpr/psum | solution.py:12
  252.2 7.9 collective-permute-done
  260.9 7.6 collective-permute-done.1
  268.6 8.1 collective-permute-done.2
  290.8 73.0 %all-reduce.2.cloned.1.call-done = f32[1024,512]{1,0:T(8,128)} async-done(((f32[1024,512]{1,0:T(8,128)}), f32[1024,512]{1,0:T(8,128)}) %all-reduce.2.cloned.1.call-update) | async-done | bytes 2097168 | tf_op jit(solution)/shard_map/while/body/eval_jaxpr/psum | solution.py:12
  380.9 7.3 collective-permute-done.1
  388.3 8.1 collective-permute-done.2
  410.5 68.8 %all-reduce.2.cloned.1.call-done = f32[1024,512]{1,0:T(8,128)} async-done(((f32[1024,512]{1,0:T(8,128)}), f32[1024,512]{1,0:T(8,128)}) %all-reduce.2.cloned.1.call-update) | async-done | bytes 2097168 | tf_op jit(solution)/shard_map/while/body/eval_jaxpr/psum | solution.py:12
  503.9 8.1 collective-permute-done.2
  526.0 74.0 %all-reduce.2.cloned.1.call-done = f32[1024,512]{1,0:T(8,128)} async-done(((f32[1024,512]{1,0:T(8,128)}), f32[1024,512]{1,0:T(8,128)}) %all-reduce.2.cloned.1.call-update) | async-done | bytes 2097168 | tf_op jit(solution)/shard_map/while/body/eval_jaxpr/psum | solution.py:12
  624.6 8.1 collective-permute-done.2
  646.8 68.9 %all-reduce.2.cloned.1.call-done = f32[1024,512]{1,0:T(8,128)} async-done(((f32[1024,512]{1,0:T(8,128)}), f32[1024,512]{1,0:T(8,128)}) %all-reduce.2.cloned.1.call-update) | async-done | bytes 2097168 | tf_op jit(solution)/shard_map/while/body/eval_jaxpr/psum | solution.py:12
  740.2 8.1 collective-permute-done.2
  762.4 75.1 %all-reduce.2.cloned.1.call-done = f32[1024,512]{1,0:T(8,128)} async-done(((f32[1024,512]{1,0:T(8,128)}), f32[1024,512]{1,0:T(8,128)}) %all-reduce.2.cloned.1.call-update) | async-done | bytes 2097168 | tf_op jit(solution)/shard_map/while/body/eval_jaxpr/psum | solution.py:12
  862.1 8.1 collective-permute-done.2
  884.3 70.0 %all-reduce.2.cloned.1.call-done = f32[1024,512]{1,0:T(8,128)} async-done(((f32[1024,512]{1,0:T(8,128)}), f32[1024,512]{1,0:T(8,128)}) %all-reduce.2.cloned.1.call-update) | async-done | bytes 2097168 | tf_op jit(solution)/shard_map/while/body/eval_jaxpr/psum | solution.py:12
  (287 shorter events, 307.8 us)
Async XLA Ops:
  11.4 117.2 %all-reduce.2.cloned.1.call-start = ((), (), s32[]{:S(2)}) async-start(), calls=%async_computation | async-start | bytes 4194304 | tf_op jit(solution)/shard_map/while/body/eval_jaxpr/psum | solution.py:12
  12.4 11.4 %collective-permute-start = (f32[128,512]{1,0:T(8,128)S(1)}, f32[128,512]{1,0:T(8,128)S(1)}, u32[]{:S(2)}, u32[]{:S(2)}) collective-permute-start(f32[128,512]{1,0:T(8,128)S(1)} %dynamic-slice_bitcast_fusion.2), channel_id=1, source_target_pairs={{0,1},{1,2},{2,3},{3,0},{4,5},{5,6},{6,7},{7,4},{8,9},{9,10},{10,1... | collective-permute-start | bytes 786440 | tf_op jit(solution)/shard_map/while/body/eval_jaxpr/ppermute | solution.py:41
  23.8 9.3 collective-permute-start.1
  33.1 8.4 collective-permute-start.2
  135.9 107.2 %all-reduce.2.cloned.1.call-start = ((), (), s32[]{:S(2)}) async-start(), calls=%async_computation | async-start | bytes 4194304 | tf_op jit(solution)/shard_map/while/body/eval_jaxpr/psum | solution.py:12
  136.9 8.2 collective-permute-start
  145.1 8.2 collective-permute-start.1
  153.3 8.2 collective-permute-start.2
  249.7 114.0 %all-reduce.2.cloned.1.call-start = ((), (), s32[]{:S(2)}) async-start(), calls=%async_computation | async-start | bytes 4194304 | tf_op jit(solution)/shard_map/while/body/eval_jaxpr/psum | solution.py:12
  250.7 9.4 collective-permute-start
  260.1 8.5 collective-permute-start.1
  268.5 8.2 collective-permute-start.2
  370.4 108.9 %all-reduce.2.cloned.1.call-start = ((), (), s32[]{:S(2)}) async-start(), calls=%async_computation | async-start | bytes 4194304 | tf_op jit(solution)/shard_map/while/body/eval_jaxpr/psum | solution.py:12
  371.4 8.7 collective-permute-start
  380.1 8.2 collective-permute-start.1
  388.3 8.2 collective-permute-start.2
  485.9 114.1 %all-reduce.2.cloned.1.call-start = ((), (), s32[]{:S(2)}) async-start(), calls=%async_computation | async-start | bytes 4194304 | tf_op jit(solution)/shard_map/while/body/eval_jaxpr/psum | solution.py:12
  486.9 8.7 collective-permute-start
  606.7 109.0 %all-reduce.2.cloned.1.call-start = ((), (), s32[]{:S(2)}) async-start(), calls=%async_computation | async-start | bytes 4194304 | tf_op jit(solution)/shard_map/while/body/eval_jaxpr/psum | solution.py:12
  607.7 8.7 collective-permute-start
  722.3 115.3 %all-reduce.2.cloned.1.call-start = ((), (), s32[]{:S(2)}) async-start(), calls=%async_computation | async-start | bytes 4194304 | tf_op jit(solution)/shard_map/while/body/eval_jaxpr/psum | solution.py:12
  723.3 8.7 collective-permute-start
  844.2 110.2 %all-reduce.2.cloned.1.call-start = ((), (), s32[]{:S(2)}) async-start(), calls=%async_computation | async-start | bytes 4194304 | tf_op jit(solution)/shard_map/while/body/eval_jaxpr/psum | solution.py:12
  845.2 8.7 collective-permute-start
  (25 other events, 93.0 us)
Sparse Core Ops, SparseCore 0:
  71.0 57.6 all-reduce.1
  175.6 67.4 all-reduce.1
  290.9 72.8 all-reduce.1
  410.6 68.6 all-reduce.1
  526.1 73.8 all-reduce.1
  646.9 68.7 all-reduce.1
  762.5 74.9 all-reduce.1
  884.4 69.8 all-reduce.1
